TPU v7x, 512 devices: a whole 4x8x8 slice. The times are simulated.
512 devices in a mesh: seq: 16 (over z, core), dp: 8 (over y), mp: 4 (over x).
Axes of the slice: x: 4, y: 8, z: 8, core: 2. Of those that a mesh axis runs over, the one named last changes fastest.
Arguments:
- features: bfloat16 [8, 4096, 8, 512], P('dp', 'seq', None, 'mp'), may hold values from -6 to 6
- key_projection: bfloat16 [8, 4096, 8, 128], P('dp', 'seq'), may hold values from -2 to 2
- query_proj: bfloat16 [8, 4096, 8, 128], P('dp', 'seq'), may hold values from -2 to 2
- step_raw: float32 [8, 4096, 8, 8], P('dp', 'seq', None, 'mp'), may hold values from -3 to 6
- doc_starts: int32 [8, 4096], P('dp', 'seq'), may hold values 0 or 1
- log_rate: float32 [8, 8], P(None, 'mp'), may hold values from -5 to 1
- step_bias: float32 [8, 8], P(None, 'mp'), may hold values from -5 to -2.5
- skip_gain: float32 [8, 8], P(None, 'mp'), may hold values from 0.5 to 1.5
- out_grad: bfloat16 [8, 4096, 8, 512], P('dp', 'seq', None, 'mp'), may hold values from -6 to 6
Outputs:
- mixed_out: bfloat16 [8, 4096, 8, 512], P('dp', 'seq', None, 'mp')
- features_grad: bfloat16 [8, 4096, 8, 512], P('dp', 'seq', None, 'mp')
- key_grad: bfloat16 [8, 4096, 8, 128], P('dp', 'seq', 'mp')
- query_grad: bfloat16 [8, 4096, 8, 128], P('dp', 'seq', 'mp')
- step_grad: float32 [8, 4096, 8, 8], P('dp', 'seq', None, 'mp')
- log_rate_grad: float32 [8, 8], P(None, 'mp')
- step_bias_grad: float32 [8, 8], P(None, 'mp')
- skip_grad: float32 [8, 8], P(None, 'mp')
All inputs are finite; a program needn't handle non-finite values. No bound on the sum of `doc_starts` on one device may be relied on, other than what follows from the above.
Results may differ from a plain program's by a relative error of at most 0.0015.
Values sent between devices are 32-bit elements; how exact they have to be, the bound alone decides.
No kernel may reach another device: no remote copies, remote signals or barrier semaphores. Data moves between devices by JAX's collectives and lax.ppermute only.
A program may use at most 128 MiB of HBM per device.

v0:
```python
import math

import jax
import jax.numpy as jnp
from jax import lax
from jax.sharding import PartitionSpec as P

P_SIZE = 64


triple = lax.Precision.HIGH


def prefix(shard, axis, combine, identity, reverse):
    length, position = (lax.axis_size(axis), lax.axis_index(axis))
    everything = jax.tree.map(lambda part: lax.all_gather(part, axis), shard)
    start = jax.tree.map(
        lambda part, zero: jnp.broadcast_to(jnp.asarray(zero, part.dtype), part.shape),
        shard,
        identity,
    )

    def step(k, before):
        at = length - 1 - k if reverse else k
        reached = at > position if reverse else at < position
        new = combine(before, jax.tree.map(lambda part: part[at], everything))
        return jax.tree.map(lambda a, b: jnp.where(reached, a, b), new, before)

    return lax.fori_loop(0, length, step, start)


def decay_terms(step_raw, doc_starts, log_rate, step_bias):
    step_size = jax.nn.softplus(step_raw + step_bias)
    log_decay = -step_size * jnp.exp(log_rate)
    cumulative = jnp.cumsum(log_decay, axis=1)
    doc_count = jnp.cumsum(doc_starts, axis=1)
    return (step_size, cumulative, doc_count)


def block_forward(
    head_vals, key_vals, query_vals, step_raw, doc_starts, log_rate, step_bias, skip_gain, state_in
):
    step_size, cumulative, doc_count = decay_terms(step_raw, doc_starts, log_rate, step_bias)
    block_len = head_vals.shape[1]
    causal = jnp.arange(block_len)[:, None] >= jnp.arange(block_len)[None, :]
    same_doc = causal[None] & (doc_count[:, :, None] == doc_count[:, None, :])
    doc_mask = same_doc[..., None, None]
    gap_log = cumulative[:, :, None] - cumulative[:, None, :]
    decay_mat = jnp.where(doc_mask, jnp.exp(jnp.where(doc_mask, gap_log, 0.0)), 0.0)
    entry_decay = jnp.where((doc_count == 0)[:, :, None, None], jnp.exp(cumulative), 0.0)
    scores = jnp.einsum("rtgn,rsgn->rtsg", query_vals, key_vals, precision=triple)
    mixing = scores[..., None] * decay_mat * step_size[:, None]
    output = jnp.einsum("rtsgh,rsghp->rtghp", mixing, head_vals, precision=triple)
    output = (
        output
        + jnp.einsum("rtgn,rghpn->rtghp", query_vals, state_in, precision=triple)
        * entry_decay[..., None]
    )
    output = output + skip_gain[..., None] * head_vals
    last_decay = decay_mat[:, -1]
    state_out = state_in * entry_decay[:, -1][..., None, None]
    state_out = state_out + jnp.einsum(
        "rsgh,rsghp,rsgn->rghpn", last_decay * step_size, head_vals, key_vals, precision=triple
    )
    return (output, state_out)


def block_summary(head_vals, key_vals, step_raw, doc_starts, log_rate, step_bias):
    step_size, cumulative, doc_count = decay_terms(step_raw, doc_starts, log_rate, step_bias)
    tail_doc = (doc_count == doc_count[:, -1:])[:, :, None, None]
    last_decay = jnp.where(
        tail_doc, jnp.exp(jnp.where(tail_doc, cumulative[:, -1:] - cumulative, 0.0)), 0.0
    )
    passed_forward = jnp.where(
        (doc_count[:, -1] == 0)[:, None, None], jnp.exp(cumulative[:, -1]), 0.0
    )
    summary_state = jnp.einsum(
        "rsgh,rsghp,rsgn->rghpn", last_decay * step_size, head_vals, key_vals, precision=triple
    )
    return (passed_forward, summary_state)


def forward_combine(earlier, trailing_portion):
    return (
        earlier[0] * trailing_portion[0],
        trailing_portion[0][..., None, None] * earlier[1] + trailing_portion[1],
    )


def backward_combine(earlier, trailing_portion):
    return (
        earlier[0] * trailing_portion[0],
        trailing_portion[1] + trailing_portion[0][..., None, None] * earlier[1],
    )


def local(
    features,
    key_projection,
    query_proj,
    step_raw,
    doc_starts,
    log_rate,
    step_bias,
    skip_gain,
    out_grad,
):
    row_count, length, groups, feat_width = features.shape
    head_count = feat_width // P_SIZE
    block_len = math.gcd(length, 128)
    block_count = length // block_len
    head_vals = features.astype(jnp.float32).reshape(row_count, length, groups, head_count, P_SIZE)
    key_vals = key_projection.astype(jnp.float32)
    query_vals = query_proj.astype(jnp.float32)
    passed_forward, summary_state = block_summary(
        head_vals, key_vals, step_raw, doc_starts, log_rate, step_bias
    )
    state_in = prefix(
        (passed_forward, summary_state),
        "seq",
        forward_combine,
        (jnp.ones_like(passed_forward), jnp.zeros_like(summary_state)),
        False,
    )[1]

    def to_blocks(array):
        return jnp.moveaxis(
            array.reshape((row_count, block_count, block_len) + array.shape[2:]), 1, 0
        )

    def local_layer(
        head_vals, key_vals, query_vals, step_raw, log_rate, step_bias, skip_gain, state_in
    ):

        def stepper(state, pieces):
            vals_b, keys_b, queries_b, raw_b, starts_b = pieces
            output, new_state = block_forward(
                vals_b, keys_b, queries_b, raw_b, starts_b, log_rate, step_bias, skip_gain, state
            )
            return (new_state, output)

        final_state, block_outs = lax.scan(
            jax.checkpoint(stepper),
            state_in,
            (
                to_blocks(head_vals),
                to_blocks(key_vals),
                to_blocks(query_vals),
                to_blocks(step_raw),
                to_blocks(doc_starts),
            ),
        )
        outputs = jnp.moveaxis(block_outs, 0, 1).reshape(
            row_count, length, groups, head_count, P_SIZE
        )
        return (outputs, final_state)

    primal, pullback = jax.vjp(
        local_layer,
        head_vals,
        key_vals,
        query_vals,
        step_raw,
        log_rate,
        step_bias,
        skip_gain,
        state_in,
    )
    mixed_vals = primal[0]
    cotangent = out_grad.astype(jnp.float32).reshape(head_vals.shape)
    _, cumulative, doc_count = decay_terms(step_raw, doc_starts, log_rate, step_bias)
    entry_decay = jnp.where((doc_count == 0)[:, :, None, None], jnp.exp(cumulative), 0.0)
    adjoint_local = jnp.einsum(
        "rtgh,rtghp,rtgn->rghpn", entry_decay, cotangent, query_vals, precision=triple
    )
    adjoint_in = prefix(
        (passed_forward, adjoint_local),
        "seq",
        backward_combine,
        (jnp.ones_like(passed_forward), jnp.zeros_like(adjoint_local)),
        True,
    )[1]
    gradients = pullback((cotangent, adjoint_in))
    vals_grad, keys_grad, queries_grad, raw_grad, rate_grad, bias_grad, gain_grad, _ = gradients
    key_part, query_part = (
        lax.psum_scatter(keys_grad, "mp", scatter_dimension=2, tiled=True),
        lax.psum_scatter(queries_grad, "mp", scatter_dimension=2, tiled=True),
    )
    rate_total, bias_total, gain_total = lax.psum((rate_grad, bias_grad, gain_grad), ("seq", "dp"))
    return (
        mixed_vals.reshape(features.shape).astype(jnp.bfloat16),
        vals_grad.reshape(features.shape).astype(jnp.bfloat16),
        key_part.astype(jnp.bfloat16),
        query_part.astype(jnp.bfloat16),
        raw_grad,
        rate_total,
        bias_total,
        gain_total,
    )


def solution(mesh):
    return jax.shard_map(
        local,
        mesh=mesh,
        in_specs=(
            P("dp", "seq", None, "mp"),
            P("dp", "seq", None, None),
            P("dp", "seq", None, None),
            P("dp", "seq", None, "mp"),
            P("dp", "seq"),
            P(None, "mp"),
            P(None, "mp"),
            P(None, "mp"),
            P("dp", "seq", None, "mp"),
        ),
        out_specs=(
            P("dp", "seq", None, "mp"),
            P("dp", "seq", None, "mp"),
            P("dp", "seq", "mp", None),
            P("dp", "seq", "mp", None),
            P("dp", "seq", None, "mp"),
            P(None, "mp"),
            P(None, "mp"),
            P(None, "mp"),
        ),
        check_vma=False,
    )
```

profile of v0, /device:TPU:6, one launch (start us, length us, event | category | flops | bytes accessed | tf_op | source)
XLA Modules:
  0.0 560.5 jit_solution(17976242943628089828)
XLA Ops:
  15.7 2.3 fusion.127
  24.7 2.1 copy.470
  26.8 2.1 copy.469
  30.1 23.6 %all_gather.18 = f32[16,1,8,2]{2,3,1,0:T(2,128)S(1)} all-gather(f32[1,1,8,2]{2,3,1,0:T(2,128)S(1)} %copy.462), channel_id=1, replica_groups=mesh['seq'=16,'dp'=8,'mp'=4] {'seq'}, dimensions={0}, use_global_device_ids=true | all-gather | bytes 1088 | tf_op jit(solution)/shard_map/all_gather | solution.py:16
  53.7 28.4 %all-gather.7.cloned.1.call-done = f32[128,2,64,128]{3,2,1,0:T(8,128)} async-done(((f32[8,2,64,128]{3,2,1,0:T(8,128)}), f32[128,2,64,128]{3,2,1,0:T(8,128)}) %all-gather.7.cloned.1.call-update) | async-done | bytes 8388624 | tf_op jit(solution)/shard_map/all_gather | solution.py:16
  82.1 20.8 %while.78 = (s32[]{:T(128)}, f32[1,8,2,64,128]{4,3,2,1,0:T(8,128)S(1)}, s32[]{:T(128)}, f32[16,1,8,2,64,128]{5,4,3,2,1,0:T(8,128)}, f32[16,1,8,2]{2,3,1,0:T(2,12...) while((s32[]{:T(128)}, f32[1,8,2,64,128]{4,3,2,1,0:T(8,128)S(1)}, s32[]{:T(128)}, ...), condition=%wide.region_11.12_spmd.clone, body=%wide.region_10.11_spmd.clone.sunk | while | flops 524296 | bytes 1573359 | solution.py:29
  102.9 39.2 %all-gather.5.cloned.1.call-done = f32[128,2,64,128]{3,2,1,0:T(8,128)} async-done(((f32[8,2,64,128]{3,2,1,0:T(8,128)}), f32[128,2,64,128]{3,2,1,0:T(8,128)}) %all-gather.5.cloned.1.call-update) | async-done | bytes 8388624 | tf_op jit(solution)/shard_map/all_gather | solution.py:16
  142.1 20.6 %while.77 = (s32[]{:T(128)}, f32[1,8,2,64,128]{4,3,2,1,0:T(8,128)S(1)}, s32[]{:T(128)}, f32[16,1,8,2]{2,3,1,0:T(2,128)S(1)}, f32[16,1,8,2,64,128]{5,4,3,2,1,0:T(8,128)}, /*index=5*/s32[]{:T(128)}, s32[]{:T(128)}) while((s32[]{:T(128)}, f32[1,8,2,64,128]{4,3,2,1,0:T(8,128)S(1)}, s32[]{:T(128)}, f32[16,1,8,2]{2,3,1,0:T(2,128)S(1)}, ...), condition=%wide.region_5.6_spmd.clone, body=%wide.region_4.5_spmd.clone.sunk | while | flops 524292 | bytes 1573297 | solution.py:29
  163.6 30.4 %while.76 = (s32[]{:T(128)}, f32[1,8,2,64,128]{4,3,2,1,0:T(8,128)S(1)}, bf16[2,1,128,8,2,64]{2,5,4,3,1,0:T(8,128)(2,1)}, f32[2,1,8,2,64,128]{5,4,3,2,1,0:T(8,128...) while((s32[]{:T(128)}, ...), condition=%wide.region_9.10_spmd.clone, body=%wide.region_6.9_spmd.clone.sunk | while | flops 405264384 | bytes 14427908 | solution.py:142
  168.5 1.8 fusion.210
  170.3 1.9 convolution_bitcast_fusion.16
  173.1 3.3 fusion.211
  183.6 1.8 fusion.210
  185.5 1.9 convolution_bitcast_fusion.16
  188.3 3.3 fusion.211
  197.8 90.8 %while.79 = (s32[]{:T(128)}, f32[8,2]{1,0:T(8,128)}, f32[8,2]{0,1:T(2,128)}, f32[8,2]{1,0:T(8,128)}, f32[1,8,2,64,128]{4,3,2,1,0:T(8,128)S(1)}, /*index=5*/bf16[...) while((s32[]{:T(128)}, f32[8,2]{1,0:T(8,128)}, ...), condition=%wide.region_25.26_spmd.clone, body=%wide.region_12.25_spmd.clone.sunk | while | flops 1015154816 | bytes 36794436 | solution.py:142
  198.4 1.8 constant_dynamic-slice_fusion.4
  208.8 2.0 copy.623
  210.9 2.0 copy.612
  220.5 1.6 convolution_bitcast_fusion.19
  223.1 3.3 fusion.239
  229.7 1.9 fusion.242
  235.6 2.7 fusion.245
  243.2 1.8 constant_dynamic-slice_fusion.4
  254.2 2.0 copy.623
  256.3 2.0 copy.612
  268.6 3.3 fusion.239
  275.1 1.9 fusion.242
  281.7 2.7 fusion.245
  290.7 250.9 %all-reduce.2 = (f32[8,2]{0,1:T(2,128)}, f32[8,2]{0,1:T(2,128)}, f32[8,2]{0,1:T(2,128)}) all-reduce(f32[8,2]{0,1:T(2,128)} %get-tuple-element.780, f32[8,2]{0,1:T(2,128)S(1)} %copy.487, f32[8,2]{0,1:T(2,128)S(1)} %copy.488), channel_id=1, replica_groups=mesh['seq'=16,'dp'=8,'mp'=4] {'seq','dp'}, use_global_device_ids=true, to_apply=%region_28.29 | all-reduce | flops 48 | bytes 384 | tf_op jit(solution)/shard_map/psum | solution.py:189
  542.9 2.5 copy.509
  546.7 2.5 copy.512
  (326 shorter events, 146.9 us)
Async XLA Ops:
  7.2 14.6 %copy-start.4 = (f32[1,256,8,2]{1,3,2,0:T(2,128)S(1)}, f32[1,256,8,2]{1,3,2,0:T(2,128)}, u32[]{:S(2)}) copy-start(f32[1,256,8,2]{1,3,2,0:T(2,128)} %param.20) | copy-start | bytes 49156
  7.2 13.3 %copy-start.2 = (bf16[1,256,8,128]{3,2,1,0:T(8,128)(2,1)S(1)}, bf16[1,256,8,128]{3,2,1,0:T(8,128)(2,1)}, u32[]{:S(2)}) copy-start(bf16[1,256,8,128]{3,2,1,0:T(8,128)(2,1)} %param.18) | copy-start | bytes 1572868
  7.2 16.7 %copy-start.6 = (f32[8,2]{0,1:T(2,128)S(1)}, f32[8,2]{0,1:T(2,128)}, u32[]{:S(2)}) copy-start(f32[8,2]{0,1:T(2,128)} %param.24) | copy-start | bytes 196
  7.2 74.9 %all-gather.7.cloned.1.call-start = ((), (), s32[]{:S(2)}) async-start(), calls=%async_computation.5 | async-start | bytes 8912896 | tf_op jit(solution)/shard_map/all_gather | solution.py:16
  18.0 124.1 %all-gather.5.cloned.1.call-start = ((), (), s32[]{:S(2)}) async-start(), calls=%async_computation.4 | async-start | bytes 8912896 | tf_op jit(solution)/shard_map/all_gather | solution.py:16
  21.7 528.7 %reduce-scatter.5.cloned.1.call-start = ((), (), s32[]{:S(2)}) async-start(), calls=%async_computation.3 | async-start | bytes 1310720 | tf_op jit(solution)/shard_map/reduce_scatter | solution.py:187
  82.1 81.6 %copy-start.3 = (f32[8,2]{0,1:T(2,128)S(1)}, f32[8,2]{0,1:T(2,128)}, u32[]{:S(2)}) copy-start(f32[8,2]{0,1:T(2,128)} %param.23) | copy-start | bytes 196
  168.4 8.8 %copy-start.1 = (f32[2,1,128,8,2,64]{2,5,4,3,1,0:T(8,128)S(1)}, f32[2,1,128,8,2,64]{2,5,4,3,1,0:T(8,128)}, u32[]{:S(2)}) copy-start(f32[2,1,128,8,2,64]{2,5,4,3,1,0:T(8,128)} %get-tuple-element.1742) | copy-start | bytes 3145732 | tf_op jit(solution)/shard_map/jvp()/while
  183.6 8.8 %copy-start.1 = (f32[2,1,128,8,2,64]{2,5,4,3,1,0:T(8,128)S(1)}, f32[2,1,128,8,2,64]{2,5,4,3,1,0:T(8,128)}, u32[]{:S(2)}) copy-start(f32[2,1,128,8,2,64]{2,5,4,3,1,0:T(8,128)} %get-tuple-element.1742) | copy-start | bytes 3145732 | tf_op jit(solution)/shard_map/jvp()/while
  202.4 12.1 %copy-start = (f32[1,8,2,64,128]{4,3,2,1,0:T(8,128)}, f32[1,8,2,64,128]{4,3,2,1,0:T(8,128)S(1)}, u32[]{:S(2)}) copy-start(f32[1,8,2,64,128]{4,3,2,1,0:T(8,128)S(1)} %dynamic-slice_bitcast_fusion.17) | copy-start | bytes 1572868 | tf_op jit(solution)/shard_map/transpose(jvp())/while
  206.7 15.4 %copy-start.5 = (pred[128]{0:T(512)(128)(4,1)}, pred[128]{0:T(512)(128)(4,1)S(1)}, u32[]{:S(2)}) copy-start(pred[128]{0:T(512)(128)(4,1)S(1)} %broadcast_compare_fusion.5) | copy-start | bytes 388 | tf_op jit(solution)/shard_map/transpose(jvp())/while
  247.1 12.8 %copy-start = (f32[1,8,2,64,128]{4,3,2,1,0:T(8,128)}, f32[1,8,2,64,128]{4,3,2,1,0:T(8,128)S(1)}, u32[]{:S(2)}) copy-start(f32[1,8,2,64,128]{4,3,2,1,0:T(8,128)S(1)} %dynamic-slice_bitcast_fusion.17) | copy-start | bytes 1572868 | tf_op jit(solution)/shard_map/transpose(jvp())/while
  252.1 15.4 %copy-start.5 = (pred[128]{0:T(512)(128)(4,1)}, pred[128]{0:T(512)(128)(4,1)S(1)}, u32[]{:S(2)}) copy-start(pred[128]{0:T(512)(128)(4,1)S(1)} %broadcast_compare_fusion.5) | copy-start | bytes 388 | tf_op jit(solution)/shard_map/transpose(jvp())/while
  288.6 263.6 %reduce-scatter.3.cloned.1.call-start = ((), (), s32[]{:S(2)}) async-start(), calls=%async_computation.2 | async-start | bytes 1310720 | tf_op jit(solution)/shard_map/reduce_scatter | solution.py:186
Sparse Core Ops, SparseCore 0:
  18.1 63.9 all-gather.6
  84.8 57.2 all-gather.4
  288.7 24.6 reduce-scatter.4
  316.1 28.8 reduce-scatter.2
where the time goes:
time: 565 us; the launch traced here: 561 us
  blocking collectives  274 us (48%)
  local copies, waits for them, and re-layouts  81.3 us (14%)
  other arithmetic  75.2 us (13%)
  waiting for transfers between devices  68.1 us (12%)
  matrix products  44.3 us (8%)
  between operations  15.3 us (3%)
    psum x1, blocking collectives, local(): lax.psum((rate_grad, bias_grad, gain_grad), ('seq', 'dp'))  251 us
    all_gather x2, waiting for transfers between devices, prefix(): everything = jax.tree.map(lambda part: lax.all_gather(part, axis), shard)  67.6 us
    select_n x32, other arithmetic, step(): return jax.tree.map(lambda a, b: jnp.where(reached, a, b), new, before)  37.5 us
    all_gather x1, blocking collectives, prefix(): everything = jax.tree.map(lambda part: lax.all_gather(part, axis), shard)  23.6 us
    unnamed x21, local copies, waits for them, and re-layouts  17.9 us
    dot_general x6, matrix products, block_forward(): jnp.einsum('rtsgh,rsghp->rtghp', mixing, head_vals, precision=triple)  14 us
  transfers between devices with their start and end apart: 4, of which 2 were waited for; matrix products, arithmetic and copies ran while one was open for 8% of the time, Pallas kernels for 0%

commit v1 on v0

v1 whole, which is shorter than its diff:
```python
import functools

import jax
import jax.numpy as jnp
from jax import lax
from jax.experimental import pallas as pl
from jax.experimental.pallas import tpu as pltpu
from jax.sharding import PartitionSpec as P


P_SIZE = 64
N = 128
F32 = jnp.float32
BF16 = jnp.bfloat16
NN = (((1,), (0,)), ((), ()))
NT = (((1,), (1,)), ((), ()))
TN = (((0,), (0,)), ((), ()))


def dot(a, b, dims=NN):
    return lax.dot_general(a, b, dims, preferred_element_type=F32)


def split(a):
    high = a.astype(BF16)
    return high, (a - high.astype(F32)).astype(BF16)


def exact_dot(a, b):
    return lax.dot_general(
        a, b, NN, precision=lax.Precision.HIGHEST, preferred_element_type=F32
    )


def softplus(v):
    u = jnp.exp(-jnp.abs(v))
    series = u * (1.0 + u * (-1.0 / 2 + u * (1.0 / 3 + u * (-1.0 / 4 + u * (1.0 / 5)))))
    return jnp.maximum(v, 0.0) + jnp.where(u < 0.03, series, jnp.log(1.0 + u))


def pair_rows(ref, pairs, length):
    rows = [jnp.full((1, length), ref[j % 2, j // 2], F32) for j in range(pairs)]
    return jnp.concatenate(rows, axis=0)


def two_heads(rows_ref, base, g, length):
    top = rows_ref[pl.ds(base + 2 * g, 1), :]
    low = rows_ref[pl.ds(base + 2 * g + 1, 1), :]
    return jnp.concatenate(
        [jnp.broadcast_to(top, (P_SIZE, length)), jnp.broadcast_to(low, (P_SIZE, length))], axis=0
    )


CUM, DT, ENTRY, TAIL, SIG, LOGD, DOC = 0, 16, 32, 48, 64, 80, 96
ROWS = 104


def summary_kernel(
    x_hbm, dy_hbm, b_hbm, c_hbm, raw_hbm, doc_hbm, rate_hbm, bias_hbm,
    keep_ref, give_ref, rows_ref,
    xs, ys, bs, cs, x_in, dy_in, b_in, c_in, raw_ref, doc_ref, rate_ref, bias_ref, sems,
):
    length, groups, _ = x_hbm.shape
    loads = [
        pltpu.make_async_copy(src, dst, sems.at[k])
        for k, (src, dst) in enumerate((
            (raw_hbm, raw_ref), (doc_hbm, doc_ref), (rate_hbm, rate_ref), (bias_hbm, bias_ref),
            (x_hbm, x_in), (dy_hbm, dy_in), (b_hbm, b_in), (c_hbm, c_in),
        ))
    ]
    for load in loads:
        load.start()
    for load in loads[:4]:
        load.wait()
    pairs = 2 * groups
    core = core_of_chip()
    raw = jnp.concatenate([raw_ref[g] for g in range(groups)], axis=0)
    shifted = raw + pair_rows(bias_ref, pairs, length)
    dt = softplus(shifted)
    log_decay = -dt * jnp.exp(pair_rows(rate_ref, pairs, length))
    docs = jnp.broadcast_to(doc_ref[...].astype(F32), (8, length))
    before = lax.broadcasted_iota(jnp.int32, (length, length), 0)
    after = lax.broadcasted_iota(jnp.int32, (length, length), 1)
    upto = jnp.where(before <= after, 1.0, 0.0).astype(F32)
    sums = exact_dot(jnp.concatenate([log_decay, docs], axis=0), upto)
    cum = sums[:pairs]
    count = sums[pairs : pairs + 1]
    last = cum[:, length - 1 :]
    last_count = count[:, length - 1 :]
    entry = jnp.where(count == 0.0, jnp.exp(cum), 0.0)
    tail = jnp.where(count == last_count, jnp.exp(last - cum), 0.0) * dt
    rows_ref[CUM : CUM + 16] = cum
    rows_ref[DT : DT + 16] = dt
    rows_ref[ENTRY : ENTRY + 16] = entry
    rows_ref[TAIL : TAIL + 16] = tail
    rows_ref[SIG : SIG + 16] = 1.0 / (1.0 + jnp.exp(-shifted))
    rows_ref[LOGD : LOGD + 16] = log_decay
    rows_ref[DOC : DOC + 8] = jnp.broadcast_to(count, (8, length))
    for load, src, dst in zip(loads[4:], (x_in, dy_in, b_in, c_in), (xs, ys, bs, cs)):
        load.wait()
        dst[...] = src[...].astype(F32).reshape(length * groups, 128)

    def group(g, carry):
        x_t = xs[pl.ds(g, length, stride=groups), :].T
        dy_t = ys[pl.ds(g, length, stride=groups), :].T
        b_n = bs[pl.ds(g, length, stride=groups), :].astype(BF16)
        c_n = cs[pl.ds(g, length, stride=groups), :].astype(BF16)
        totals = []
        for vals, weights, other in ((x_t, TAIL, b_n), (dy_t, ENTRY, c_n)):
            high, low = split(vals * two_heads(rows_ref, weights, g, length))
            both = dot(jnp.concatenate([high, low], axis=0), other)
            totals.append(both[:128] + both[128:])

        def store(ref):
            for h in range(2):
                slot = 2 * lax.rem(g, groups // 2) + h
                passed = rows_ref[pl.ds(ENTRY + 2 * g + h, 1), :][:, length - 1 :]
                for at, total in zip((0, P_SIZE), totals):
                    ref[slot, at : at + P_SIZE] = total[h * P_SIZE : (h + 1) * P_SIZE]
                ref[slot, 2 * P_SIZE :] = jnp.broadcast_to(passed, (8, N))

        mine = g // (groups // 2) == core
        pl.when(mine)(lambda: store(keep_ref))
        pl.when(jnp.logical_not(mine))(lambda: store(give_ref))
        return carry

    lax.fori_loop(0, groups, group, 0)


def core_of_chip():
    return lax.rem(lax.axis_index("seq"), 2)


def state_of(ref, k):
    return ref[k, :P_SIZE]


def adjoint_of(ref, k):
    return ref[k, P_SIZE : 2 * P_SIZE]


def passed_of(ref, k):
    return ref[k, 2 * P_SIZE : 2 * P_SIZE + 1, :]


def chip_kernel(keep_ref, got_ref, chip_ref):
    def join(first, second):
        for k in range(chip_ref.shape[0]):
            chip_ref[k, :P_SIZE] = passed_of(second, k) * state_of(first, k) + state_of(second, k)
            chip_ref[k, P_SIZE : 2 * P_SIZE] = adjoint_of(first, k) + passed_of(
                first, k
            ) * adjoint_of(second, k)
            chip_ref[k, 2 * P_SIZE :] = first[k, 2 * P_SIZE :] * second[k, 2 * P_SIZE :]

    core = core_of_chip()
    pl.when(core == 0)(lambda: join(keep_ref, got_ref))
    pl.when(core == 1)(lambda: join(got_ref, keep_ref))


def scan_kernel(recv_ref, send_ref):
    chips = recv_ref.shape[0]
    state = jnp.zeros((P_SIZE, N), F32)
    for k in range(chips):
        send_ref[k, :P_SIZE] = state
        if k < chips - 1:
            state = passed_of(recv_ref, k) * state + state_of(recv_ref, k)
    state = jnp.zeros((P_SIZE, N), F32)
    for k in reversed(range(chips)):
        send_ref[k, P_SIZE:] = state
        if k > 0:
            state = passed_of(recv_ref, k) * state + adjoint_of(recv_ref, k)


def shard_kernel(keep_ref, got_ref, chip_ref, mine_ref, theirs_ref):
    def part(first, second, first_out, second_out):
        for k in range(chip_ref.shape[0]):
            state, adjoint = chip_ref[k, :P_SIZE], chip_ref[k, P_SIZE:]
            first_out[k, :P_SIZE] = state
            first_out[k, P_SIZE:] = passed_of(second, k) * adjoint + adjoint_of(second, k)
            second_out[k, :P_SIZE] = passed_of(first, k) * state + state_of(first, k)
            second_out[k, P_SIZE:] = adjoint

    core = core_of_chip()
    pl.when(core == 0)(lambda: part(keep_ref, got_ref, mine_ref, theirs_ref))
    pl.when(core == 1)(lambda: part(got_ref, keep_ref, theirs_ref, mine_ref))


def states_of(mine_ref, other_ref, g, groups, at):
    mine = g // (groups // 2) == core_of_chip()
    slot = 2 * lax.rem(g, groups // 2)
    return [
        jnp.where(mine, mine_ref[slot + h, at : at + P_SIZE], other_ref[slot + h, at : at + P_SIZE])
        for h in range(2)
    ]


def within_kernel(
    start,
    x_ref, dy_ref, b_ref, c_ref, rows_ref,
    yt_ref, dxt_ref, dct_ref, dbt_ref, xt_ref, dyt_ref, bt_ref, ct_ref,
    xs, ys, bs, cs,
):
    groups, _, length = yt_ref.shape
    stride = x_ref.shape[1]
    for src, dst in ((x_ref, xs), (dy_ref, ys), (b_ref, bs), (c_ref, cs)):
        dst[...] = src[...].astype(F32).reshape(length * stride, 128)
    t_at = lax.broadcasted_iota(jnp.int32, (length, length), 0)
    s_at = lax.broadcasted_iota(jnp.int32, (length, length), 1)
    count = rows_ref[DOC : DOC + 8]
    count_col = count.T[:, :1]
    far = jnp.where((t_at >= s_at) & (count_col == count[:1]), 0.0, -jnp.inf)
    lanes = lax.broadcasted_iota(jnp.int32, (length, 128), 1)

    def group(i, carry):
        g = start + i
        x_n, dy_n, b_n, c_n = (
            ref[pl.ds(g, length, stride=stride), :] for ref in (xs, ys, bs, cs)
        )
        b_t, c_t = b_n.T.astype(BF16), c_n.T.astype(BF16)
        c_n, dy_n, x_t = c_n.astype(BF16), dy_n.astype(BF16), x_n.T.astype(BF16)
        bt_ref[i] = b_t
        ct_ref[i] = c_t
        xt_ref[i] = x_t
        dyt_ref[i] = dy_n.T
        scores = dot(c_n, b_t)
        cum = jnp.concatenate(
            [rows_ref[pl.ds(CUM + 2 * g, 1), :], rows_ref[pl.ds(CUM + 2 * g + 1, 1), :]]
            + [jnp.zeros((6, length), F32)],
            axis=0,
        )
        cum_col = cum.T
        score_grad = None
        for h in range(2):
            part = slice(h * P_SIZE, (h + 1) * P_SIZE)
            dt = rows_ref[pl.ds(DT + 2 * g + h, 1), :]
            weight = jnp.exp(cum_col[:, h : h + 1] - cum[h : h + 1] + far) * dt
            high, low = split(scores * weight)
            x_h = xt_ref[i, part, :]
            dy_h = dyt_ref[i, part, :]
            yt_ref[i, part, :] = dot(x_h, high, NT) + dot(x_h, low, NT)
            dxt_ref[i, part, :] = dot(dy_h, high) + dot(dy_h, low)
            mine = (lanes < P_SIZE) if h == 0 else (lanes >= P_SIZE)
            mixing_grad = dot(jnp.where(mine, dy_n, jnp.zeros_like(dy_n)), x_t)
            score_grad = mixing_grad * weight if h == 0 else score_grad + mixing_grad * weight
        high, low = split(score_grad)
        dct_ref[i] = dot(b_t, high, NT) + dot(b_t, low, NT)
        dbt_ref[i] = dot(c_t, high) + dot(c_t, low)
        return carry

    lax.fori_loop(0, groups, group, 0)


def group_grad_kernel(
    mine_ref, other_ref, rows_ref,
    xt0_ref, xt1_ref, dyt0_ref, dyt1_ref, dct0_ref, dct1_ref, dbt0_ref, dbt1_ref,
    *send_refs,
):
    groups, _, _ = xt0_ref.shape
    groups *= 2
    owned = groups // len(send_refs)
    me = lax.axis_index("mp")

    def group(start, bases, i, carry):
        g = start + i
        totals = []
        for at, vals_ref, weights, base_ref in (
            (0, bases[0], ENTRY, bases[1]),
            (P_SIZE, bases[2], TAIL, bases[3]),
        ):
            total = base_ref[i]
            for h, state in enumerate(states_of(mine_ref, other_ref, g, groups, at)):
                high, low = split(state)
                vals = vals_ref[i, h * P_SIZE : (h + 1) * P_SIZE, :]
                grad = dot(
                    jnp.concatenate([high, low], axis=0),
                    jnp.concatenate([vals, vals], axis=0),
                    TN,
                )
                total = total + grad * rows_ref[pl.ds(weights + 2 * g + h, 1), :]
            totals.append(total)

        def store(ref):
            for which, total in enumerate(totals):
                ref[2 * lax.rem(g, owned) + which] = total

        away = lax.bitwise_xor(g // owned, me)
        for k, ref in enumerate(send_refs):
            pl.when(away == k)(functools.partial(store, ref))
        return carry

    half = groups // 2
    lax.fori_loop(0, half, functools.partial(group, 0, (dyt0_ref, dct0_ref, xt0_ref, dbt0_ref)), 0)
    lax.fori_loop(0, half, functools.partial(group, half, (dyt1_ref, dct1_ref, xt1_ref, dbt1_ref)), 0)


def finish_kernel(
    mine_ref, other_ref, rows_ref, xt0_ref, xt1_ref, dyt0_ref, dyt1_ref,
    bt0_ref, bt1_ref, ct0_ref, ct1_ref, yt0_ref, yt1_ref, dxt0_ref, dxt1_ref,
    rate_ref, gain_ref, order_ref,
    out_ref, dx_ref, raw_grad_ref, stats_ref,
    ys, dxs, through, back, skip, bound,
):
    groups, _, length = xt0_ref.shape
    groups *= 2
    pairs = 2 * groups
    both_heads = lax.broadcasted_iota(jnp.int32, (128, length), 0) < P_SIZE

    def group(start, bases, i, carry):
        g = start + i
        xt_ref, dyt_ref, bt_ref, ct_ref, yt_ref, dxt_ref = bases
        x_t, dy_t = xt_ref[i].astype(F32), dyt_ref[i].astype(F32)
        states = states_of(mine_ref, other_ref, g, groups, 0)
        adjoints = states_of(mine_ref, other_ref, g, groups, P_SIZE)

        def entering(state, other):
            high, low = split(jnp.concatenate(state, axis=0))
            return dot(
                jnp.concatenate([high, low], axis=1), jnp.concatenate([other, other], axis=0)
            )

        y_t = yt_ref[i] + entering(states, ct_ref[i]) * two_heads(rows_ref, ENTRY, g, length)
        dx_far = entering(adjoints, bt_ref[i]) * two_heads(rows_ref, TAIL, g, length)
        dx_t = dxt_ref[i] + dx_far
        gain = jnp.where(both_heads, gain_ref[0, g], gain_ref[1, g])
        ys[pl.ds(g, length, stride=groups), :] = (y_t + gain * x_t).T
        dxs[pl.ds(g, length, stride=groups), :] = (dx_t + gain * dy_t).T
        forward, backward = dy_t * y_t, x_t * dx_t
        direct, far = dy_t * x_t, x_t * dx_far
        for h in range(2):
            part = slice(h * P_SIZE, (h + 1) * P_SIZE)
            at = pl.ds(2 * g + h, 1)
            through[at, :] = jnp.sum(forward[part], axis=0, keepdims=True)
            back[at, :] = jnp.sum(backward[part], axis=0, keepdims=True)
            skip[at, :] = jnp.sum(direct[part], axis=0, keepdims=True)
            meet = jnp.sum(states[h] * adjoints[h], axis=0, keepdims=True)
            passed = rows_ref[pl.ds(ENTRY + 2 * g + h, 1), :][:, length - 1 :]
            arrive = jnp.sum(far[part], axis=0, keepdims=True)
            bound[at, :] = arrive + jnp.concatenate(
                [meet * passed, jnp.zeros((1, length - N), F32)], axis=1
            )
        return carry

    half = groups // 2
    first = (xt0_ref, dyt0_ref, bt0_ref, ct0_ref, yt0_ref, dxt0_ref)
    second = (xt1_ref, dyt1_ref, bt1_ref, ct1_ref, yt1_ref, dxt1_ref)
    lax.fori_loop(0, half, functools.partial(group, 0, first), 0)
    lax.fori_loop(0, half, functools.partial(group, half, second), 0)
    out_ref[...] = ys[...].reshape(length, groups, 128).astype(BF16)
    dx_ref[...] = dxs[...].reshape(length, groups, 128).astype(BF16)

    dt = rows_ref[DT : DT + 16]
    rate = jnp.exp(pair_rows(rate_ref, pairs, length))
    before = lax.broadcasted_iota(jnp.int32, (length, length), 0)
    after = lax.broadcasted_iota(jnp.int32, (length, length), 1)
    since = jnp.where(before >= after, 1.0, 0.0).astype(F32)
    decay_grad = exact_dot(through[...] - back[...], since)
    decay_grad = decay_grad + jnp.sum(bound[...], axis=1, keepdims=True)
    raw_grad = (back[...] / dt - rate * decay_grad) * rows_ref[SIG : SIG + 16]
    for g in range(groups):
        raw_grad_ref[g] = raw_grad[2 * g : 2 * g + 2]
    rate_grad = jnp.sum(decay_grad * rows_ref[LOGD : LOGD + 16], axis=1, keepdims=True)
    bias_grad = jnp.sum(raw_grad, axis=1, keepdims=True)
    gain_grad = jnp.sum(skip[...], axis=1, keepdims=True)
    lane = lax.broadcasted_iota(jnp.int32, (pairs, 128), 1)
    stats_ref[...] = jnp.where(
        lane == 0, rate_grad, jnp.where(lane == 1, bias_grad, jnp.where(lane == 2, gain_grad, 0.0))
    )


def gather_kernel(*refs):
    parts, (key_ref, query_ref, keys, queries) = refs[:-4], refs[-4:]
    slots, _, length = parts[0].shape
    for slot in range(slots):
        total = parts[0][slot]
        for part in parts[1:]:
            total = total + part[slot]
        dst = keys if slot % 2 else queries
        dst[pl.ds(slot // 2, length, stride=slots // 2), :] = total.T
    key_ref[...] = keys[...].reshape(key_ref.shape).astype(BF16)
    query_ref[...] = queries[...].reshape(query_ref.shape).astype(BF16)


def call(kernel, out, scratch=(), smem=(), hbm=(), flops=10**9, moved=4 << 20, vmem=24):
    def run(*args):
        spaces = [
            pltpu.SMEM if i in smem else pltpu.HBM if i in hbm else pltpu.VMEM
            for i in range(len(args))
        ]
        return pl.pallas_call(
            kernel,
            out_shape=out,
            in_specs=[pl.BlockSpec(memory_space=space) for space in spaces],
            out_specs=jax.tree.map(lambda _: pl.BlockSpec(memory_space=pltpu.VMEM), out),
            scratch_shapes=list(scratch),
            cost_estimate=pl.CostEstimate(flops=flops, bytes_accessed=moved, transcendentals=0),
            compiler_params=pltpu.CompilerParams(vmem_limit_bytes=vmem << 20),
        )(*args)

    return run


def local(
    features, key_projection, query_proj, step_raw, doc_starts, log_rate, step_bias, skip_gain,
    out_grad,
):
    _, length, groups, _ = features.shape
    pairs = 2 * groups
    half = groups // 2
    shards, owners = lax.axis_size("seq"), lax.axis_size("mp")
    shape = jax.ShapeDtypeStruct
    flat = pltpu.VMEM((length * groups, 128), F32)
    half_full = shape((half, 128, length), F32)
    half_wide = shape((half, 128, length), BF16)
    per_pair = pltpu.VMEM((pairs, length), F32)
    summary = shape((groups, 2 * P_SIZE + 8, N), F32)
    entering = shape((groups, 2 * P_SIZE, N), F32)
    rate, bias, gain = log_rate.T, step_bias.T, skip_gain.T
    partner = [(i, i ^ 1) for i in range(shards)]
    cores = [list(range(c, shards, 2)) for c in range(2)]

    def to_chips(a):
        return lax.all_to_all(a, "seq", 0, 0, axis_index_groups=cores, tiled=True)

    keep, give, rows = call(
        summary_kernel,
        (summary, summary, shape((ROWS, length), F32)),
        scratch=[flat] * 4 + [pltpu.VMEM((length, groups, 128), BF16)] * 4
        + [pltpu.VMEM((groups, 2, length), F32), pltpu.VMEM((1, length), jnp.int32)]
        + [pltpu.SMEM((2, groups), F32)] * 2 + [pltpu.SemaphoreType.DMA((8,))],
        hbm=range(8), vmem=62,
    )(features[0], out_grad[0], key_projection[0], query_proj[0],
      step_raw[0].transpose(1, 2, 0), doc_starts, rate, bias)
    got = lax.ppermute(give, "seq", partner)
    chip = call(chip_kernel, summary, vmem=60)(keep, got)
    scanned = call(scan_kernel, entering)(to_chips(chip))
    ends = to_chips(scanned)
    mine, theirs = call(shard_kernel, (entering, entering), vmem=60)(keep, got, ends)
    other = lax.ppermute(theirs, "seq", partner)
    within = [
        call(
            functools.partial(within_kernel, start),
            (half_full,) * 4 + (half_wide,) * 4, scratch=[flat] * 4, flops=10**10, vmem=60,
        )(features[0], out_grad[0], key_projection[0], query_proj[0], rows)
        for start in (0, half)
    ]
    y_in, dx_in, dc_in, db_in, x_t, dy_t, b_t, c_t = zip(*within)
    owned = groups // owners
    part = shape((2 * owned, 128, length), F32)
    grads = call(group_grad_kernel, (part,) * owners)(
        mine, other, rows, *x_t, *dy_t, *dc_in, *db_in
    )
    parts = [grads[0]]
    for k in range(1, owners):
        parts.append(lax.ppermute(grads[k], "mp", [(i, i ^ k) for i in range(owners)]))
    mixed, dx, raw_grad, stats = call(
        finish_kernel,
        (shape((length, groups, 128), BF16), shape((length, groups, 128), BF16),
         shape((groups, 2, length), F32), shape((pairs, 128), F32)),
        scratch=[flat, flat, per_pair, per_pair, per_pair, per_pair],
        smem=(15, 16), hbm=(17,), vmem=60,
    )(mine, other, rows, *x_t, *dy_t, *b_t, *c_t, *y_in, *dx_in, rate, gain, grads[0])
    stats = stats[:, :3]
    for axis in ("seq", "dp"):
        copies = jnp.broadcast_to(stats, (lax.axis_size(axis),) + stats.shape)
        copies = lax.all_to_all(copies, axis, 0, 0, tiled=True)
        stats = jnp.sum(copies, axis=0)
    out_grads = shape((length, owned, 128), BF16)
    key_grad, query_grad = call(
        gather_kernel, (out_grads, out_grads),
        scratch=[pltpu.VMEM((length * owned, 128), F32)] * 2,
    )(*parts)
    stats = stats.reshape(groups, 2, 3)
    return (
        mixed[None],
        dx[None],
        key_grad[None],
        query_grad[None],
        raw_grad.transpose(2, 0, 1)[None],
        stats[..., 0],
        stats[..., 1],
        stats[..., 2],
    )


def solution(mesh):
    return jax.shard_map(
        local,
        mesh=mesh,
        in_specs=(
            P("dp", "seq", None, "mp"),
            P("dp", "seq", None, None),
            P("dp", "seq", None, None),
            P("dp", "seq", None, "mp"),
            P("dp", "seq"),
            P(None, "mp"),
            P(None, "mp"),
            P(None, "mp"),
            P("dp", "seq", None, "mp"),
        ),
        out_specs=(
            P("dp", "seq", None, "mp"),
            P("dp", "seq", None, "mp"),
            P("dp", "seq", "mp", None),
            P("dp", "seq", "mp", None),
            P("dp", "seq", None, "mp"),
            P(None, "mp"),
            P(None, "mp"),
            P(None, "mp"),
        ),
        check_vma=False,
    )
```

time: 565 us -> 131 us (0.23)
  blocking collectives: 274 us -> 53.7 us
  other arithmetic: 75.2 us -> 0.05 us
  local copies, waits for them, and re-layouts: 81.3 us -> 9.36 us
  waiting for transfers between devices: 68.1 us -> 11.9 us
  matrix products: 44.3 us -> 0 us
  Pallas kernels: 0 us -> 36.9 us
  starting transfers between devices: 0.16 us -> 17.9 us
  between operations: 15.3 us -> 0.82 us
    psum x1 -> x0, blocking collectives: 251 us -> none  [local(): lax.psum((rate_grad, bias_grad, gain_grad), ('seq', 'dp'))]
    all_gather x2 -> x0, waiting for transfers between devices: 67.6 us -> none  [prefix(): everything = jax.tree.map(lambda part: lax.all_gather(part, axis), shard)]
    all_to_all x0 -> x3, blocking collectives: none -> 53.7 us  [the longest x1 28.8 us: to_chips(): return lax.all_to_all(a, 'seq', 0, 0, axis_index_groups=cores, tiled=True)]
    dot_general x30 -> x0, matrix products: 44.3 us -> none  [the longest x6 14 us: block_forward(): jnp.einsum('rtsgh,rsghp->rtghp', mixing, head_vals, precision=triple)]
    select_n x36 -> x0, other arithmetic: 40.9 us -> none  [the longest x32 37.5 us: step(): return jax.tree.map(lambda a, b: jnp.where(reached, a, b), new, before)]
    pallas_call x0 -> x9, Pallas kernels: none -> 36.9 us  [run(): pl.pallas_call(kernel, out_shape=out, in_specs=[pl.BlockSpec(memory_space...]
    all_gather x1 -> x0, blocking collectives: 23.6 us -> none  [prefix(): everything = jax.tree.map(lambda part: lax.all_gather(part, axis), shard)]
    mul x84 -> x0, local copies, waits for them, and re-layouts: 16.2 us -> none  [the longest x10 10.2 us: block_forward(): mixing = scores[..., None] * decay_mat * step_size[:, None]]
  transfers between devices with their start and end apart: 4 -> 6, of which waited for: 2 -> 2; matrix products, arithmetic and copies ran while one was open for 8% -> 2% of each run, Pallas kernels for 0% -> 16%
where the time goes in v1:
time: 131 us
  blocking collectives  53.7 us (41%)
  Pallas kernels  36.9 us (28%)
  starting transfers between devices  17.9 us (14%)
  waiting for transfers between devices  11.9 us (9%)
  local copies, waits for them, and re-layouts  9.36 us (7%)
    pallas_call x9, Pallas kernels, run(): pl.pallas_call(kernel, out_shape=out, in_specs=[pl.BlockSpec(memory_space...  36.9 us
    all_to_all x1, blocking collectives, to_chips(): return lax.all_to_all(a, 'seq', 0, 0, axis_index_groups=cores, tiled=True)  28.8 us
    all_to_all x2, blocking collectives, local(): copies = lax.all_to_all(copies, axis, 0, 0, tiled=True)  24.9 us
    ppermute x3, starting transfers between devices, local(): lax.ppermute(grads[k], 'mp', [(i, i ^ k) for i in range(owners)])  10.4 us
    all_to_all x1, waiting for transfers between devices, to_chips(): return lax.all_to_all(a, 'seq', 0, 0, axis_index_groups=cores, tiled=True)  9.76 us
    unnamed x30, local copies, waits for them, and re-layouts  6.57 us
    all_to_all x1, starting transfers between devices, to_chips(): return lax.all_to_all(a, 'seq', 0, 0, axis_index_groups=cores, tiled=True)  3.49 us
  transfers between devices with their start and end apart: 6, of which 2 were waited for; matrix products, arithmetic and copies ran while one was open for 2% of the time, Pallas kernels for 16%

profile of v1, /device:TPU:6, one launch (start us, length us, event | category | flops | bytes accessed | tf_op | source)
XLA Modules:
  0.0 130.6 jit_solution(159071847879177860)
XLA Ops:
  0.6 6.7 %shard_map.152 = (f32[8,136,128]{2,1,0:T(8,128)}, f32[8,136,128]{2,1,0:T(8,128)}, f32[104,256]{1,0:T(8,128)}) custom-call(bf16[256,8,128]{2,1,0:T(8,128)(2,1)} %bitcast.30, bf16[256,8,128]{2,1,0:T(8,128)(2,1)} %bitcast.33, bf16[256,8,128]{2,1,0:T(8,128)(2,1)} %bitcast.36, bf16[256,8,128]{2,1,0:T(8,128)(2,1)} %bitcast.39, f32[8,2,256]{2,1,0:T(2,128)} %bitcast.44, ...), custom_call_target="tpu_custom_call" | custom-call | flops 1000000000 | bytes 4194304 | tf_op jit(solution)/shard_map/pallas_call | solution.py:389
  7.4 1.9 %collective-permute-start = (f32[8,136,128]{2,1,0:T(8,128)}, f32[8,136,128]{2,1,0:T(8,128)S(1)}, u32[]{:S(2)}, u32[]{:S(2)}) collective-permute-start(f32[8,136,128]{2,1,0:T(8,128)} %get-tuple-element.40), channel_id=1, source_target_pairs={{0,32},{32,0},{64,96},{96,64},{128,160},{160,128},{192,224},{224,1... | collective-permute-start | bytes 1671176 | tf_op jit(solution)/shard_map/ppermute | solution.py:433
  9.3 2.1 %collective-permute-done.got_ref = f32[8,136,128]{2,1,0:T(8,128)S(1)} collective-permute-done((f32[8,136,128]{2,1,0:T(8,128)}, f32[8,136,128]{2,1,0:T(8,128)S(1)}, u32[]{:S(2)}, u32[]{:S(2)}) %collective-permute-start) | collective-permute-done | bytes 557088 | tf_op jit(solution)/shard_map/ppermute | solution.py:433
  11.4 0.8 copy-done.14
  12.3 2.1 %shard_map.153 = f32[8,136,128]{2,1,0:T(8,128)} custom-call(f32[8,136,128]{2,1,0:T(8,128)} %get-tuple-element.39.keep_ref, f32[8,136,128]{2,1,0:T(8,128)} %copy-done.14), custom_call_target="tpu_custom_call" | custom-call | flops 1000000000 | bytes 4194304 | tf_op jit(solution)/shard_map/pallas_call | solution.py:389
  14.3 28.8 %all_to_all.20.recv_ref = f32[8,136,128]{2,1,0:T(8,128)S(1)} all-to-all(f32[8,136,128]{2,1,0:T(8,128)} %shard_map.153), channel_id=1, replica_groups={{0,64,128,192,256,320,384,448},{32,96,160,224,288,352,416,480},{1,65,12..., dimensions={0} | all-to-all | bytes 1114112 | tf_op jit(solution)/shard_map/all_to_all | solution.py:422
  43.2 0.8 shard_map.154
  44.0 3.5 %all-to-all-start.1 = ((f32[8,128,128]{2,1,0:T(8,128)}), f32[8,128,128]{2,1,0:T(8,128)S(1)}, u32[]{:S(2)}, u32[]{:S(2)}) async-start(f32[8,128,128]{2,1,0:T(8,128)} %shard_map.154), calls=%async_computation.1 | async-start | bytes 1048576 | tf_op jit(solution)/shard_map/all_to_all | solution.py:422
  47.5 7.2 %shard_map.157 = (f32[4,128,256]{2,1,0:T(8,128)}, f32[4,128,256]{2,1,0:T(8,128)}, f32[4,128,256]{2,1,0:T(8,128)}, f32[4,128,256]{2,1,0:T(8,128)}, bf16[4,128,256...) custom-call(bf16[256,8,128]{2,1,0:T(8,128)(2,1)} %bitcast.31, ...), custom_call_target="tpu_custom_call" | custom-call | flops 10000000000 | bytes 4194304 | tf_op jit(solution)/shard_map/pallas_call | solution.py:389
  54.6 9.8 %all-to-all-done.1.chip_ref = f32[8,128,128]{2,1,0:T(8,128)S(1)} async-done(((f32[8,128,128]{2,1,0:T(8,128)}), f32[8,128,128]{2,1,0:T(8,128)S(1)}, u32[]{:S(2)}, u32[]{:S(2)}) %all-to-all-start.1) | async-done | bytes 524320 | tf_op jit(solution)/shard_map/all_to_all | solution.py:422
  64.4 0.8 copy-done.13
  65.2 2.4 %shard_map.155 = (f32[8,128,128]{2,1,0:T(8,128)}, f32[8,128,128]{2,1,0:T(8,128)}) custom-call(f32[8,136,128]{2,1,0:T(8,128)} %get-tuple-element.39.keep_ref, f32[8,136,128]{2,1,0:T(8,128)} %copy-done.14, f32[8,128,128]{2,1,0:T(8,128)} %copy-done.13), custom_call_target="tpu_custom_call" | custom-call | flops 1000000000 | bytes 4194304 | tf_op jit(solution)/shard_map/pallas_call | solution.py:389
  67.7 2.1 %collective-permute-start.1 = (f32[8,128,128]{2,1,0:T(8,128)}, f32[8,128,128]{2,1,0:T(8,128)S(1)}, u32[]{:S(2)}, u32[]{:S(2)}) collective-permute-start(f32[8,128,128]{2,1,0:T(8,128)} %get-tuple-element.42), channel_id=1, source_target_pairs={{0,32},{32,0},{64,96},{96,64},{128,160},{160,128},{192,224},{224,1... | collective-permute-start | bytes 1572872 | tf_op jit(solution)/shard_map/ppermute | solution.py:438
  69.7 7.1 %shard_map.156 = (f32[4,128,256]{2,1,0:T(8,128)}, f32[4,128,256]{2,1,0:T(8,128)}, f32[4,128,256]{2,1,0:T(8,128)}, f32[4,128,256]{2,1,0:T(8,128)}, bf16[4,128,256...) custom-call(bf16[256,8,128]{2,1,0:T(8,128)(2,1)} %bitcast.32, ...), custom_call_target="tpu_custom_call" | custom-call | flops 10000000000 | bytes 4194304 | tf_op jit(solution)/shard_map/pallas_call | solution.py:389
  76.9 1.1 copy-done.4
  78.0 0.9 copy-done.5
  79.0 1.0 copy-done.10
  80.0 1.0 copy-done.11
  81.0 3.2 %shard_map.158 = (f32[4,128,256]{2,1,0:T(8,128)S(1)}, f32[4,128,256]{2,1,0:T(8,128)}, f32[4,128,256]{2,1,0:T(8,128)S(1)}, f32[4,128,256]{2,1,0:T(8,128)S(1)}) custom-call(f32[8,128,128]{2,1,0:T(8,128)S(1)} %copy-done, f32[8,128,128]{2,1,0:T(8,128)S(1)} %collective-permute-done.1.other_ref, f32[104,256]{1,0:T(8,128)S(1)} %copy-done.12, ...), custom_call_target="tpu_custom_call" | custom-call | flops 1000000000 | bytes 4194304 | tf_op jit(solution)/shard_map/pallas_call | solution.py:389
  84.2 0.8 copy-done.6
  85.0 2.7 %collective-permute-start.2 = (f32[4,128,256]{2,1,0:T(8,128)}, f32[4,128,256]{2,1,0:T(8,128)S(1)}, u32[]{:S(2)}, u32[]{:S(2)}) collective-permute-start(f32[4,128,256]{2,1,0:T(8,128)} %get-tuple-element.63), channel_id=1, source_target_pairs={{0,1},{1,0},{2,3},{3,2},{4,5},{5,4},{6,7},{7,6},{8,9},{9,8},{10,11... | collective-permute-start | bytes 1572872 | tf_op jit(solution)/shard_map/ppermute | solution.py:454
  87.7 3.0 %collective-permute-start.3 = (f32[4,128,256]{2,1,0:T(8,128)S(1)}, f32[4,128,256]{2,1,0:T(8,128)S(1)}, u32[]{:S(2)}, u32[]{:S(2)}) collective-permute-start(f32[4,128,256]{2,1,0:T(8,128)S(1)} %get-tuple-element.64), channel_id=1, source_target_pairs={{0,2},{1,3},{2,0},{3,1},{4,6},{5,7},{6,4},{7,5},{8,10},{9,11},{10,... | collective-permute-start | bytes 1572872 | tf_op jit(solution)/shard_map/ppermute | solution.py:454
  90.8 4.7 %collective-permute-start.4 = (f32[4,128,256]{2,1,0:T(8,128)S(1)}, f32[4,128,256]{2,1,0:T(8,128)S(1)}, u32[]{:S(2)}, u32[]{:S(2)}) collective-permute-start(f32[4,128,256]{2,1,0:T(8,128)S(1)} %get-tuple-element.65), channel_id=1, source_target_pairs={{0,3},{1,2},{2,1},{3,0},{4,7},{5,6},{6,5},{7,4},{8,11},{9,10},{10,... | collective-permute-start | bytes 1572872 | tf_op jit(solution)/shard_map/ppermute | solution.py:454
  95.5 6.4 %shard_map.159 = (bf16[256,8,128]{2,1,0:T(8,128)(2,1)}, bf16[256,8,128]{2,1,0:T(8,128)(2,1)}, f32[8,2,256]{2,1,0:T(2,128)}, f32[16,128]{1,0:T(8,128)}) custom-call(f32[8,128,128]{2,1,0:T(8,128)} %get-tuple-element.41.mine_ref, f32[8,128,128]{2,1,0:T(8,128)} %copy-done.1, f32[104,256]{1,0:T(8,128)} %get-tuple-element.43.rows_ref, ...), custom_call_target="tpu_custom_call" | custom-call | flops 1000000000 | bytes 4194304 | tf_op jit(solution)/shard_map/pallas_call | solution.py:389
  101.8 0.8 copy.23
  102.6 10.3 %all_to_all.21 = f32[16,16,3]{1,2,0:T(4,128)S(1)} all-to-all(f32[16,16,3]{1,2,0:T(4,128)S(1)} %broadcast_in_dim.26), channel_id=1, replica_groups=mesh['seq'=16,'dp'=8,'mp'=4] {'seq'}, dimensions={0} | all-to-all | bytes 6144 | tf_op jit(solution)/shard_map/all_to_all | solution.py:465
  112.9 14.7 %all_to_all.22 = f32[8,16,3]{1,2,0:T(4,128)S(1)} all-to-all(f32[8,16,3]{1,2,0:T(4,128)S(1)} %broadcast_in_dim.27), channel_id=1, replica_groups=mesh['seq'=16,'dp'=8,'mp'=4] {'dp'}, dimensions={0} | all-to-all | bytes 3072 | tf_op jit(solution)/shard_map/all_to_all | solution.py:465
  127.6 0.1 reshape.19
  127.7 0.6 copy.26
  128.3 0.6 copy.25
  128.9 0.6 copy.24
  129.6 1.0 shard_map.160
  (32 shorter events, 0.1 us)
Async XLA Ops:
  7.4 4.1 %collective-permute-start = (f32[8,136,128]{2,1,0:T(8,128)}, f32[8,136,128]{2,1,0:T(8,128)S(1)}, u32[]{:S(2)}, u32[]{:S(2)}) collective-permute-start(f32[8,136,128]{2,1,0:T(8,128)} %get-tuple-element.40), channel_id=1, source_target_pairs={{0,32},{32,0},{64,96},{96,64},{128,160},{160,128},{192,224},{224,1... | collective-permute-start | bytes 1671176 | tf_op jit(solution)/shard_map/ppermute | solution.py:433
  11.4 0.8 copy-start.14
  44.0 20.4 %all-to-all-start.1 = ((f32[8,128,128]{2,1,0:T(8,128)}), f32[8,128,128]{2,1,0:T(8,128)S(1)}, u32[]{:S(2)}, u32[]{:S(2)}) async-start(f32[8,128,128]{2,1,0:T(8,128)} %shard_map.154), calls=%async_computation.1 | async-start | bytes 1048576 | tf_op jit(solution)/shard_map/all_to_all | solution.py:422
  64.4 0.8 copy-start.13
  67.6 9.2 %copy-start = (f32[8,128,128]{2,1,0:T(8,128)S(1)}, f32[8,128,128]{2,1,0:T(8,128)}, u32[]{:S(2)}) copy-start(f32[8,128,128]{2,1,0:T(8,128)} %get-tuple-element.41.mine_ref) | copy-start | bytes 1572868
  67.6 9.2 %copy-start.2 = (bf16[4,128,256]{2,1,0:T(8,128)(2,1)S(1)}, bf16[4,128,256]{2,1,0:T(8,128)(2,1)}, u32[]{:S(2)}) copy-start(bf16[4,128,256]{2,1,0:T(8,128)(2,1)} %get-tuple-element.45.xt1_ref) | copy-start | bytes 786436
  67.6 9.3 %copy-start.3 = (bf16[4,128,256]{2,1,0:T(8,128)(2,1)S(1)}, bf16[4,128,256]{2,1,0:T(8,128)(2,1)}, u32[]{:S(2)}) copy-start(bf16[4,128,256]{2,1,0:T(8,128)(2,1)} %get-tuple-element.47.dyt1_ref) | copy-start | bytes 786436
  67.6 9.3 %copy-start.8 = (f32[4,128,256]{2,1,0:T(8,128)S(1)}, f32[4,128,256]{2,1,0:T(8,128)}, u32[]{:S(2)}) copy-start(f32[4,128,256]{2,1,0:T(8,128)} %get-tuple-element.57.dct1_ref) | copy-start | bytes 1572868
  67.6 9.3 %copy-start.9 = (f32[4,128,256]{2,1,0:T(8,128)S(1)}, f32[4,128,256]{2,1,0:T(8,128)}, u32[]{:S(2)}) copy-start(f32[4,128,256]{2,1,0:T(8,128)} %get-tuple-element.59.dbt1_ref) | copy-start | bytes 1572868
  67.6 9.3 %copy-start.12 = (f32[104,256]{1,0:T(8,128)S(1)}, f32[104,256]{1,0:T(8,128)}, u32[]{:S(2)}) copy-start(f32[104,256]{1,0:T(8,128)} %get-tuple-element.43.rows_ref) | copy-start | bytes 319492
  67.7 9.2 %collective-permute-start.1 = (f32[8,128,128]{2,1,0:T(8,128)}, f32[8,128,128]{2,1,0:T(8,128)S(1)}, u32[]{:S(2)}, u32[]{:S(2)}) collective-permute-start(f32[8,128,128]{2,1,0:T(8,128)} %get-tuple-element.42), channel_id=1, source_target_pairs={{0,32},{32,0},{64,96},{96,64},{128,160},{160,128},{192,224},{224,1... | collective-permute-start | bytes 1572872 | tf_op jit(solution)/shard_map/ppermute | solution.py:438
  76.8 7.4 %copy-start.1 = (f32[8,128,128]{2,1,0:T(8,128)}, f32[8,128,128]{2,1,0:T(8,128)S(1)}, u32[]{:S(2)}) copy-start(f32[8,128,128]{2,1,0:T(8,128)S(1)} %collective-permute-done.1.other_ref) | copy-start | bytes 1572868
  76.9 1.1 copy-start.4
  78.0 0.9 copy-start.5
  79.0 1.0 copy-start.10
  80.0 1.0 copy-start.11
  84.2 0.8 copy-start.6
  85.0 44.6 %collective-permute-start.2 = (f32[4,128,256]{2,1,0:T(8,128)}, f32[4,128,256]{2,1,0:T(8,128)S(1)}, u32[]{:S(2)}, u32[]{:S(2)}) collective-permute-start(f32[4,128,256]{2,1,0:T(8,128)} %get-tuple-element.63), channel_id=1, source_target_pairs={{0,1},{1,0},{2,3},{3,2},{4,5},{5,4},{6,7},{7,6},{8,9},{9,8},{10,11... | collective-permute-start | bytes 1572872 | tf_op jit(solution)/shard_map/ppermute | solution.py:454
  87.7 41.8 %collective-permute-start.3 = (f32[4,128,256]{2,1,0:T(8,128)S(1)}, f32[4,128,256]{2,1,0:T(8,128)S(1)}, u32[]{:S(2)}, u32[]{:S(2)}) collective-permute-start(f32[4,128,256]{2,1,0:T(8,128)S(1)} %get-tuple-element.64), channel_id=1, source_target_pairs={{0,2},{1,3},{2,0},{3,1},{4,6},{5,7},{6,4},{7,5},{8,10},{9,11},{10,... | collective-permute-start | bytes 1572872 | tf_op jit(solution)/shard_map/ppermute | solution.py:454
  90.8 38.8 %collective-permute-start.4 = (f32[4,128,256]{2,1,0:T(8,128)S(1)}, f32[4,128,256]{2,1,0:T(8,128)S(1)}, u32[]{:S(2)}, u32[]{:S(2)}) collective-permute-start(f32[4,128,256]{2,1,0:T(8,128)S(1)} %get-tuple-element.65), channel_id=1, source_target_pairs={{0,3},{1,2},{2,1},{3,0},{4,7},{5,6},{6,5},{7,4},{8,11},{9,10},{10,... | collective-permute-start | bytes 1572872 | tf_op jit(solution)/shard_map/ppermute | solution.py:454
  95.4 34.1 %copy-start.7 = (f32[4,128,256]{2,1,0:T(8,128)S(1)}, f32[4,128,256]{2,1,0:T(8,128)}, u32[]{:S(2)}) copy-start(f32[4,128,256]{2,1,0:T(8,128)} %copy-done.6) | copy-start | bytes 1572868
